TPU v7x, 256 devices: a whole 4x4x8 slice. The times are simulated.
256 devices in a mesh: row: 32 (over x, y, z_lo), src: 8 (over z_hi, core).
Axes of the slice: x: 4, y: 4, z: 8 (z_hi: 4, z_lo: 2; z = z_hi * 2 + z_lo), core: 2. Of those that a mesh axis runs over, the one named last changes fastest.
Arguments:
- traces: bfloat16 [16384, 128, 512], P('row', 'src'), may hold values from -6 to 6
- row_source: int32 [16384], P('row'), may hold values from 0 to 16383, as said below
- slice_data: bfloat16 [2, 16384, 32, 512], P(None, 'row', None, 'src'), may hold values from -0.03125 to 0.03125
- wavelet_inverse: float32 [2], replicated, may hold values from 0.3 to 0.8
Outputs:
- multiples: float32 [16384, 2, 128], P(('row', 'src'))
- primaries: float32 [16384, 2, 128], P(('row', 'src'))
Inputs may be any that keep to these rules, and one draw needn't show every extreme that they name: `row_source`: every recording row is named exactly once; entry e * 512 + p names a recording row whose index modulo 512 lies in [e * 16, (e + 1) * 16).
All inputs are finite; a program needn't handle non-finite values.
Results may differ from a plain program's by a relative error of at most 0.0056.
Values may be sent and summed in bfloat16 or wider, within the bound.
A program may use at most 64 MiB of HBM per device.

v0:
```python
import jax
import jax.numpy as jnp
from jax import lax
from jax.sharding import PartitionSpec as P

FREQ = 61
ITERS = 3


def dft_kernel(samples):
    ticks = jnp.arange(samples, dtype=jnp.int32)
    moment = ticks.astype(jnp.float32)
    ramp_len = samples // 8
    rising = 0.5 - 0.5 * jnp.cos(jnp.pi * (moment + 0.5) / ramp_len)
    falling = 0.5 - 0.5 * jnp.cos(jnp.pi * (samples - moment - 0.5) / ramp_len)
    taper = jnp.where(
        ticks < ramp_len,
        rising,
        jnp.where(ticks >= samples - ramp_len, falling, jnp.ones_like(rising)),
    )
    wrapped = ticks * FREQ % samples
    angles = 2.0 * jnp.pi / samples * wrapped.astype(jnp.float32)
    factor = 1.0 / jnp.sqrt(jnp.float32(samples))
    table = jnp.stack([taper * jnp.cos(angles) * factor, -taper * jnp.sin(angles) * factor], axis=1)
    return table.astype(jnp.bfloat16)


def combine_parts(real_terms, imag_terms, shot_count):
    pred_real = real_terms[:, :shot_count] - imag_terms[:, shot_count:]
    pred_imag = real_terms[:, shot_count:] + imag_terms[:, :shot_count]
    return jnp.stack([pred_real, pred_imag], axis=1)


def body(traces, row_source, slice_data, wavelet_inverse):
    block_rows, shot_local, samples = traces.shape
    kernel = dft_kernel(samples)
    spectra = jnp.dot(
        traces.reshape(block_rows * shot_local, samples), kernel, preferred_element_type=jnp.float32
    )
    spectra = jnp.transpose(spectra.reshape(block_rows, shot_local, 2), (0, 2, 1)).astype(
        jnp.bfloat16
    )
    arrived = lax.all_to_all(spectra, "row", split_axis=0, concat_axis=0, tiled=True)
    group_rows = block_rows // lax.axis_size("row")
    located = row_source // block_rows * group_rows + row_source % group_rows
    ordered = arrived[located]
    slice_rows = block_rows // lax.axis_size("src")
    panel = lax.all_to_all(ordered, "src", split_axis=0, concat_axis=2, tiled=True)
    shot_count = panel.shape[2]
    base = panel.astype(jnp.float32)
    wave_real = wavelet_inverse[0]
    wave_imag = wavelet_inverse[1]
    real_data = slice_data[0].reshape(block_rows, -1)
    imag_data = slice_data[1].reshape(block_rows, -1)
    estimate = panel
    predicted = jnp.zeros((slice_rows, 2, shot_count), jnp.float32)
    primaries = base
    for iteration in range(ITERS):
        shard_rows = lax.all_gather(estimate, "row", axis=0, tiled=True)
        piece_rows = shard_rows.shape[0]
        stacked = shard_rows.reshape(piece_rows, 2 * shot_count)
        real_terms = jnp.dot(real_data, stacked, preferred_element_type=jnp.float32)
        imag_terms = jnp.dot(imag_data, stacked, preferred_element_type=jnp.float32)
        summed = lax.psum(combine_parts(real_terms, imag_terms, shot_count), "src")
        predicted = lax.dynamic_slice_in_dim(
            summed, lax.axis_index("src") * slice_rows, slice_rows, 0
        )
        next_real = base[:, 0] - (wave_real * predicted[:, 0] - wave_imag * predicted[:, 1])
        next_imag = base[:, 1] - (wave_real * predicted[:, 1] + wave_imag * predicted[:, 0])
        primaries = jnp.stack([next_real, next_imag], axis=1)
        estimate = primaries.astype(jnp.bfloat16)
    return (predicted, primaries)


def solution(mesh):
    in_specs = (P("row", "src", None), P("row"), P(None, "row", None, "src"), P())
    out_specs = (P(("row", "src"), None, None), P(("row", "src"), None, None))
    return jax.shard_map(body, mesh=mesh, in_specs=in_specs, out_specs=out_specs, check_vma=False)
```

profile of v0, /device:TPU:2, one launch (start us, length us, event | category | flops | bytes accessed | tf_op | source)
XLA Modules:
  0.0 753.8 jit_solution(3112653908474504425)
XLA Ops:
  7.3 5.6 fusion
  13.5 0.9 reshape.153
  14.3 9.0 %all-to-all-start = ((bf16[32,2,256]{2,1,0:T(2,128)(2,1)}), bf16[32,2,256]{2,1,0:T(2,128)(2,1)S(1)}, u32[]{:S(2)}, u32[]{:S(2)}) async-start(bf16[32,2,256]{2,1,0:T(2,128)(2,1)} %reshape.153), calls=%async_computation | async-start | bytes 65536 | tf_op jit(solution)/shard_map/all_to_all | solution.py:43
  23.4 7.0 all-to-all-done
  30.6 2.1 gather_fusion
  33.0 15.2 %all_to_all.23 = bf16[8,2,1024]{2,1,0:T(2,128)(2,1)S(1)} all-to-all(bf16[8,2,1024]{2,1,0:T(2,128)(2,1)S(1)} %reshape.155), channel_id=1, replica_groups=mesh['row'=32,'src'=8] {'src'}, dimensions={0} | all-to-all | bytes 65536 | tf_op jit(solution)/shard_map/all_to_all | solution.py:48
  49.4 4.0 fusion.41
  53.4 136.0 %all-gather.4.cloned.1.call-done = bf16[2048,2,128]{2,1,0:T(2,128)(2,1)} async-done(((bf16[64,2,128]{2,1,0:T(2,128)(2,1)}), bf16[2048,2,128]{2,1,0:T(2,128)(2,1)}) %all-gather.4.cloned.1.call-update) | async-done | bytes 1048592 | tf_op jit(solution)/shard_map/all_gather | solution.py:59
  189.4 2.7 convolution_bitcast_fusion.4
  192.1 0.7 convolution_bitcast_fusion.5
  193.0 0.8 pad_maximum_fusion
  194.5 80.9 %all-reduce.4.cloned.1.call-done = f32[512,2,128]{0,2,1:T(8,128)} async-done(((f32[512,2,128]{0,2,1:T(8,128)}), f32[512,2,128]{0,2,1:T(8,128)}) %all-reduce.4.cloned.1.call-update) | async-done | bytes 524304 | tf_op jit(solution)/shard_map/psum | solution.py:64
  275.5 2.1 subtract_convert_fusion.3
  278.4 144.4 %all-gather.6.cloned.1.call-done = bf16[2048,2,128]{2,1,0:T(2,128)(2,1)} async-done(((bf16[64,2,128]{2,1,0:T(2,128)(2,1)}), bf16[2048,2,128]{2,1,0:T(2,128)(2,1)}) %all-gather.6.cloned.1.call-update) | async-done | bytes 1048592 | tf_op jit(solution)/shard_map/all_gather | solution.py:59
  422.9 2.7 convolution_bitcast_fusion.2
  426.5 0.8 pad_maximum_fusion.1
  427.4 81.5 %all-reduce.6.cloned.1.call-done = f32[512,2,128]{0,2,1:T(8,128)} async-done(((f32[512,2,128]{0,2,1:T(8,128)}), f32[512,2,128]{0,2,1:T(8,128)}) %all-reduce.6.cloned.1.call-update) | async-done | bytes 524304 | tf_op jit(solution)/shard_map/psum | solution.py:64
  508.8 2.1 subtract_convert_fusion.1
  511.8 144.4 %all-gather.8.cloned.1.call-done = bf16[2048,2,128]{2,1,0:T(2,128)(2,1)} async-done(((bf16[64,2,128]{2,1,0:T(2,128)(2,1)}), bf16[2048,2,128]{2,1,0:T(2,128)(2,1)}) %all-gather.8.cloned.1.call-update) | async-done | bytes 1048592 | tf_op jit(solution)/shard_map/all_gather | solution.py:59
  656.3 2.7 convolution_bitcast_fusion
  659.8 0.8 pad_maximum_fusion.2
  660.7 81.6 %all-reduce.8.cloned.1.call-done = f32[512,2,128]{0,2,1:T(8,128)} async-done(((f32[512,2,128]{0,2,1:T(8,128)}), f32[512,2,128]{0,2,1:T(8,128)}) %all-reduce.8.cloned.1.call-update) | async-done | bytes 524304 | tf_op jit(solution)/shard_map/psum | solution.py:64
  742.3 1.0 constant_dynamic-slice_fusion
  744.0 2.1 subtract_subtract_fusion
  (46 shorter events, 7.9 us)
Async XLA Ops:
  7.3 16.1 %copy-start = (s32[512]{0:T(512)S(1)}, s32[512]{0:T(512)}, u32[]{:S(2)}) copy-start(s32[512]{0:T(512)} %param.5) | copy-start | bytes 6148
  14.3 16.1 %all-to-all-start = ((bf16[32,2,256]{2,1,0:T(2,128)(2,1)}), bf16[32,2,256]{2,1,0:T(2,128)(2,1)S(1)}, u32[]{:S(2)}, u32[]{:S(2)}) async-start(bf16[32,2,256]{2,1,0:T(2,128)(2,1)} %reshape.153), calls=%async_computation | async-start | bytes 65536 | tf_op jit(solution)/shard_map/all_to_all | solution.py:43
  23.3 166.1 %all-gather.4.cloned.1.call-start = ((), (), s32[]{:S(2)}) async-start(), calls=%async_computation.2 | async-start | bytes 1081344 | tf_op jit(solution)/shard_map/all_gather | solution.py:59
  49.4 226.1 %all-reduce.4.cloned.1.call-start = ((), (), s32[]{:S(2)}) async-start(), calls=%async_computation.3 | async-start | bytes 1048576 | tf_op jit(solution)/shard_map/psum | solution.py:64
  189.4 2.7 copy-start.2
  192.9 1.0 copy-start.1
  193.9 229.0 %all-gather.6.cloned.1.call-start = ((), (), s32[]{:S(2)}) async-start(), calls=%async_computation.4 | async-start | bytes 1081344 | tf_op jit(solution)/shard_map/all_gather | solution.py:59
  278.4 230.5 %all-reduce.6.cloned.1.call-start = ((), (), s32[]{:S(2)}) async-start(), calls=%async_computation.5 | async-start | bytes 1048576 | tf_op jit(solution)/shard_map/psum | solution.py:64
  422.9 2.7 copy-start.4
  427.3 229.0 %all-gather.8.cloned.1.call-start = ((), (), s32[]{:S(2)}) async-start(), calls=%async_computation.6 | async-start | bytes 1081344 | tf_op jit(solution)/shard_map/all_gather | solution.py:59
  511.8 230.6 %all-reduce.8.cloned.1.call-start = ((), (), s32[]{:S(2)}) async-start(), calls=%async_computation.7 | async-start | bytes 1048576 | tf_op jit(solution)/shard_map/psum | solution.py:64
  656.3 2.7 copy-start.3
Sparse Core Ops, SparseCore 0:
  49.5 139.8 all-gather.3
  194.0 81.4 all-reduce.3
  278.5 144.3 all-gather.5
  427.4 81.3 all-reduce.5
  511.9 144.3 all-gather.7
  660.8 81.4 all-reduce.7
where the time goes:
time: 754 us
  waiting for transfers between devices  676 us (90%)
  matrix products  16 us (2%)
  blocking collectives  15.2 us (2%)
  between operations  14.4 us (2%)
  local copies, waits for them, and re-layouts  13.5 us (2%)
  other arithmetic  9.38 us (1%)
  starting transfers between devices  9.22 us (1%)
    all_gather x3, waiting for transfers between devices, body(): shard_rows = lax.all_gather(estimate, 'row', axis=0, tiled=True)  425 us
    psum x3, waiting for transfers between devices, body(): summed = lax.psum(combine_parts(real_terms, imag_terms, shot_count), 'src')  244 us
    all_to_all x1, blocking collectives, body(): lax.all_to_all(ordered, 'src', split_axis=0, concat_axis=2, tiled=True)  15.2 us
  transfers between devices with their start and end apart: 7, of which 7 were waited for; matrix products, arithmetic and copies ran while one was open for 1% of the time, Pallas kernels for 0%

commit v1 on v0

--- a/solution.py
+++ b/solution.py
@@ -61,7 +61,9 @@
         stacked = shard_rows.reshape(piece_rows, 2 * shot_count)
         real_terms = jnp.dot(real_data, stacked, preferred_element_type=jnp.float32)
         imag_terms = jnp.dot(imag_data, stacked, preferred_element_type=jnp.float32)
-        summed = lax.psum(combine_parts(real_terms, imag_terms, shot_count), "src")
+        summed = jnp.sum(
+            lax.all_gather(combine_parts(real_terms, imag_terms, shot_count), "src"), axis=0
+        )
         predicted = lax.dynamic_slice_in_dim(
             summed, lax.axis_index("src") * slice_rows, slice_rows, 0
         )

time: 754 us -> 722 us (0.958)
  waiting for transfers between devices: 676 us -> 611 us
  local copies, waits for them, and re-layouts: 13.5 us -> 36.7 us
    psum x3 -> x0, waiting for transfers between devices: 244 us -> none  [body(): summed = lax.psum(combine_parts(real_terms, imag_terms, shot_count), 'src')]
    all_gather x0 -> x3, waiting for transfers between devices: none -> 177 us  [body(): lax.all_gather(combine_parts(real_terms, imag_terms, shot_count), 'src')]
    unnamed x16 -> x19, local copies, waits for them, and re-layouts: 3.02 us -> 27 us
    reduce_sum x0 -> x3, other arithmetic: none -> 9.56 us  [body(): jnp.sum(lax.all_gather(combine_parts(real_terms, imag_terms, shot_count),...]
where the time goes in v1:
time: 722 us; the launch traced here: 719 us
  waiting for transfers between devices  611 us (85%)
  local copies, waits for them, and re-layouts  36.7 us (5%)
  other arithmetic  16.8 us (2%)
  matrix products  16 us (2%)
  blocking collectives  15.2 us (2%)
  between operations  14.4 us (2%)
  starting transfers between devices  9.62 us (1%)
    all_gather x3, waiting for transfers between devices, body(): shard_rows = lax.all_gather(estimate, 'row', axis=0, tiled=True)  426 us
    all_gather x3, waiting for transfers between devices, body(): lax.all_gather(combine_parts(real_terms, imag_terms, shot_count), 'src')  177 us
    unnamed x19, local copies, waits for them, and re-layouts  27 us
    all_to_all x1, blocking collectives, body(): lax.all_to_all(ordered, 'src', split_axis=0, concat_axis=2, tiled=True)  15.2 us
  transfers between devices with their start and end apart: 7, of which 7 were waited for; matrix products, arithmetic and copies ran while one was open for 1% of the time, Pallas kernels for 0%

profile of v1, /device:TPU:2, one launch (start us, length us, event | category | flops | bytes accessed | tf_op | source)
XLA Modules:
  0.0 719.3 jit_solution(4921269796708357343)
XLA Ops:
  7.3 5.6 fusion
  14.3 9.0 %all-to-all-start = ((bf16[32,2,256]{2,1,0:T(2,128)(2,1)}), bf16[32,2,256]{2,1,0:T(2,128)(2,1)S(1)}, u32[]{:S(2)}, u32[]{:S(2)}) async-start(bf16[32,2,256]{2,1,0:T(2,128)(2,1)} %reshape.156), calls=%async_computation | async-start | bytes 65536 | tf_op jit(solution)/shard_map/all_to_all | solution.py:43
  23.4 7.0 all-to-all-done
  30.6 2.1 gather_fusion
  33.0 15.2 %all_to_all.23 = bf16[8,2,1024]{2,1,0:T(2,128)(2,1)S(1)} all-to-all(bf16[8,2,1024]{2,1,0:T(2,128)(2,1)S(1)} %reshape.158), channel_id=1, replica_groups=mesh['row'=32,'src'=8] {'src'}, dimensions={0} | all-to-all | bytes 65536 | tf_op jit(solution)/shard_map/all_to_all | solution.py:48
  49.4 4.0 fusion.41
  53.5 135.9 %all-gather.10.cloned.1.call-done = bf16[2048,2,128]{2,1,0:T(2,128)(2,1)} async-done(((bf16[64,2,128]{2,1,0:T(2,128)(2,1)}), bf16[2048,2,128]{2,1,0:T(2,128)(2,1)}) %all-gather.10.cloned.1.call-update) | async-done | bytes 1048592 | tf_op jit(solution)/shard_map/all_gather | solution.py:59
  189.4 2.7 convolution_bitcast_fusion.4
  194.6 58.5 %all-gather.16.cloned.1.call-done = f32[4096,2,128]{0,2,1:T(8,128)} async-done(((f32[512,2,128]{0,2,1:T(8,128)}), f32[4096,2,128]{0,2,1:T(8,128)}) %all-gather.16.cloned.1.call-update) | async-done | bytes 4194320 | tf_op jit(solution)/shard_map/all_gather | solution.py:65
  253.1 8.0 %copy.19 = f32[32,8,8,512]{3,2,1,0:T(8,128)} copy(f32[32,8,8,512]{3,1,2,0:T(8,128)} %bitcast.88) | data formatting | bytes 8388608
  261.1 3.2 reduce_sum.27
  264.3 1.4 subtract_convert_fusion.3
  266.8 145.2 %all-gather.12.cloned.1.call-done = bf16[2048,2,128]{2,1,0:T(2,128)(2,1)} async-done(((bf16[64,2,128]{2,1,0:T(2,128)(2,1)}), bf16[2048,2,128]{2,1,0:T(2,128)(2,1)}) %all-gather.12.cloned.1.call-update) | async-done | bytes 1048592 | tf_op jit(solution)/shard_map/all_gather | solution.py:59
  412.0 2.7 convolution_bitcast_fusion.2
  416.5 59.3 %all-gather.18.cloned.1.call-done = f32[4096,2,128]{0,2,1:T(8,128)} async-done(((f32[512,2,128]{0,2,1:T(8,128)}), f32[4096,2,128]{0,2,1:T(8,128)}) %all-gather.18.cloned.1.call-update) | async-done | bytes 4194320 | tf_op jit(solution)/shard_map/all_gather | solution.py:65
  475.7 8.0 %copy.21 = f32[32,8,8,512]{3,2,1,0:T(8,128)} copy(f32[32,8,8,512]{3,1,2,0:T(8,128)} %bitcast.89) | data formatting | bytes 8388608
  483.7 3.2 reduce_sum.28
  486.9 1.4 subtract_convert_fusion.1
  489.4 145.2 %all-gather.14.cloned.1.call-done = bf16[2048,2,128]{2,1,0:T(2,128)(2,1)} async-done(((bf16[64,2,128]{2,1,0:T(2,128)(2,1)}), bf16[2048,2,128]{2,1,0:T(2,128)(2,1)}) %all-gather.14.cloned.1.call-update) | async-done | bytes 1048592 | tf_op jit(solution)/shard_map/all_gather | solution.py:59
  634.6 2.7 convolution_bitcast_fusion
  639.0 59.3 %all-gather.20.cloned.1.call-done = f32[4096,2,128]{0,2,1:T(8,128)} async-done(((f32[512,2,128]{0,2,1:T(8,128)}), f32[4096,2,128]{0,2,1:T(8,128)}) %all-gather.20.cloned.1.call-update) | async-done | bytes 4194320 | tf_op jit(solution)/shard_map/all_gather | solution.py:65
  698.3 8.0 %copy.23 = f32[32,8,8,512]{3,2,1,0:T(8,128)} copy(f32[32,8,8,512]{3,1,2,0:T(8,128)} %bitcast.90) | data formatting | bytes 8388608
  706.3 3.2 reduce_sum.29
  709.5 1.4 subtract_subtract_fusion
  (52 shorter events, 12.5 us)
Async XLA Ops:
  7.3 16.1 %copy-start = (s32[512]{0:T(512)S(1)}, s32[512]{0:T(512)}, u32[]{:S(2)}) copy-start(s32[512]{0:T(512)} %param.5) | copy-start | bytes 6148
  14.3 16.1 %all-to-all-start = ((bf16[32,2,256]{2,1,0:T(2,128)(2,1)}), bf16[32,2,256]{2,1,0:T(2,128)(2,1)S(1)}, u32[]{:S(2)}, u32[]{:S(2)}) async-start(bf16[32,2,256]{2,1,0:T(2,128)(2,1)} %reshape.156), calls=%async_computation | async-start | bytes 65536 | tf_op jit(solution)/shard_map/all_to_all | solution.py:43
  23.3 166.1 %all-gather.10.cloned.1.call-start = ((), (), s32[]{:S(2)}) async-start(), calls=%async_computation.2 | async-start | bytes 1081344 | tf_op jit(solution)/shard_map/all_gather | solution.py:59
  49.4 203.8 %all-gather.16.cloned.1.call-start = ((), (), s32[]{:S(2)}) async-start(), calls=%async_computation.5 | async-start | bytes 4718592 | tf_op jit(solution)/shard_map/all_gather | solution.py:65
  189.4 2.7 copy-start.2
  192.9 1.0 copy-start.1
  193.9 218.1 %all-gather.12.cloned.1.call-start = ((), (), s32[]{:S(2)}) async-start(), calls=%async_computation.3 | async-start | bytes 1081344 | tf_op jit(solution)/shard_map/all_gather | solution.py:59
  266.5 209.2 %all-gather.18.cloned.1.call-start = ((), (), s32[]{:S(2)}) async-start(), calls=%async_computation.6 | async-start | bytes 4718592 | tf_op jit(solution)/shard_map/all_gather | solution.py:65
  412.0 2.7 copy-start.4
  416.4 218.2 %all-gather.14.cloned.1.call-start = ((), (), s32[]{:S(2)}) async-start(), calls=%async_computation.4 | async-start | bytes 1081344 | tf_op jit(solution)/shard_map/all_gather | solution.py:59
  489.1 209.2 %all-gather.20.cloned.1.call-start = ((), (), s32[]{:S(2)}) async-start(), calls=%async_computation.7 | async-start | bytes 4718592 | tf_op jit(solution)/shard_map/all_gather | solution.py:65
  634.6 2.7 copy-start.3
Sparse Core Ops, SparseCore 0:
  49.5 139.8 all-gather.9
  194.0 59.1 all-gather.15
  266.7 145.2 all-gather.11
  416.5 59.1 all-gather.17
  489.3 145.2 all-gather.13
  639.2 59.1 all-gather.19
